TPU v7x, 32 devices: a whole 2x2x4 slice. The times are simulated.
32 devices in a mesh: ctx: 8 (over z, y), tp: 4 (over x, core).
Axes of the slice: x: 2, y: 2, z: 4, core: 2. Of those that a mesh axis runs over, the one named last changes fastest.
Arguments:
- qkv: bfloat16 [1024, 3, 8192], P(('ctx', 'tp')), may hold values from -6 to 6
- filters: float32 [3, 7, 8192], P(None, None, 'tp'), may hold values from -1.5 to 1.5
- doc_ids: int32 [8], replicated, may hold values from 0 to 1, never falling along the last dimension, each value on 1 to 5 neighbouring positions
- upstream: bfloat16 [1024, 8192], P('ctx', 'tp'), may hold values from -6 to 6
Outputs:
- attended: bfloat16 [1024, 8192], P('ctx', 'tp')
- qkv_grad: bfloat16 [1024, 3, 8192], P(('ctx', 'tp'))
- filter_grad: float32 [3, 7, 8192], P(None, None, 'tp')
Inputs may be any that keep to these rules, and one draw needn't show every extreme that they name: doc_ids never falls along the sequence; every document covers 1 to 5 whole blocks of 128 tokens.
All inputs are finite; a program needn't handle non-finite values.
Results may differ from a plain program's by a relative error of at most 0.014.
The roundings to bfloat16 on the way count: a program that leaves them out, or rounds other values in their place, can miss the bound.
Values may be sent and summed in bfloat16 or wider, within the bound.
No kernel may reach another device: no remote copies, remote signals or barrier semaphores. Data moves between devices by JAX's collectives and lax.ppermute only.
A program may use at most 128 MiB of HBM per device.

v0:
```python
import functools
import math

import jax
import jax.numpy as jnp
from jax import lax
from jax.experimental import pallas as pl
from jax.experimental.pallas import tpu as pltpu
from jax.sharding import PartitionSpec as P

HEAD_DIM = 128
KW = 7
BLOCK = 128
STEPS = 4
PAD = 8
SCALE = HEAD_DIM ** (-0.5)
SCALE_LOG2 = SCALE * math.log2(math.e)
AXES = ("ctx", "tp")
FORE, BACK, SPREAD = 24, 24, 16


def dot(a, b, dims):
    return lax.dot_general(a, b, (dims, ((), ())), preferred_element_type=jnp.float32)


def room(mebibytes):
    return pltpu.CompilerParams(vmem_limit_bytes=mebibytes << 20)


def estimate(flops, moved):
    return pl.CostEstimate(flops=flops, bytes_accessed=moved, transcendentals=0)


def split_columns(x, members, tp, mebibytes):
    streams, rows, channels = x.shape
    width = channels // tp // members
    steps = 2 if tp % 2 == 0 else 1
    part = tp // steps

    def kernel(x_ref, o_ref):
        for t in range(part):
            for c in range(members):
                at = (t * members + c) * width
                o_ref[c, t] = x_ref[:, :, at : at + width]

    return pl.pallas_call(
        kernel,
        grid=(steps,),
        in_specs=[pl.BlockSpec((streams, rows, part * members * width), lambda i: (0, 0, i))],
        out_specs=pl.BlockSpec((members, part, streams, rows, width), lambda i: (0, i, 0, 0, 0)),
        out_shape=jax.ShapeDtypeStruct((members, tp, streams, rows, width), x.dtype),
        cost_estimate=estimate(0, 4 * x.size),
        compiler_params=room(mebibytes),
        name="split_columns",
    )(x)


def split_rows(x, members, local):
    tokens, channels = x.shape
    width = channels // members

    def kernel(local_ref, x_ref, *o_refs):
        for step in range(members):
            at = pl.multiple_of((local_ref[0] ^ step) * width, width)
            o_refs[step][...] = x_ref[:, pl.ds(at, width)]

    piece = pl.BlockSpec((tokens, width), lambda i, p: (0, 0))
    return pl.pallas_call(
        kernel,
        grid_spec=pltpu.PrefetchScalarGridSpec(
            num_scalar_prefetch=1,
            grid=(1,),
            in_specs=[pl.BlockSpec((tokens, channels), lambda i, p: (0, 0))],
            out_specs=[piece] * members,
        ),
        out_shape=[jax.ShapeDtypeStruct((tokens, width), x.dtype)] * members,
        compiler_params=room(10),
        cost_estimate=estimate(0, 4 * x.size),
        name="split_rows",
    )(local, x)


def join_columns(x):
    members, tp, streams, rows, width = x.shape
    steps = 2 if tp % 2 == 0 else 1
    part = tp // steps

    def kernel(x_ref, o_ref):
        for t in range(part):
            for c in range(members):
                at = (t * members + c) * width
                o_ref[:, :, at : at + width] = x_ref[c, pl.program_id(0) * part + t]

    return pl.pallas_call(
        kernel,
        grid=(steps,),
        in_specs=[pl.BlockSpec(memory_space=pltpu.VMEM)],
        out_specs=pl.BlockSpec((streams, rows, part * members * width), lambda i: (0, 0, i)),
        out_shape=pltpu.HBM((streams, rows, tp * members * width), x.dtype),
        cost_estimate=estimate(0, 4 * x.size),
        compiler_params=room(10),
        name="join_columns",
    )(x)


def tile_starts(tokens):
    starts, total = [], 0
    for block in range(tokens // BLOCK):
        starts.append(total)
        total += block + 1 - max(0, block - STEPS)
    return starts, total


def row_groups(tokens):
    blocks = tokens // BLOCK
    size = 2 if blocks % 2 == 0 else 1
    for start in range(0, blocks, size):
        yield range(start, start + size), max(0, start - STEPS)


def widened(value, block, group, first):
    before = (max(0, block - STEPS) - first) * BLOCK
    behind = (group[-1] - block) * BLOCK
    parts = [jnp.zeros((BLOCK, before), value.dtype)] if before else []
    parts.append(value)
    if behind:
        parts.append(jnp.zeros((BLOCK, behind), value.dtype))
    return jnp.concatenate(parts, axis=1) if len(parts) > 1 else value


def stacked(parts):
    return jnp.concatenate(parts, axis=0) if len(parts) > 1 else parts[0]


def forward_kernel(docs, x_ref, taps_ref, before_ref, mixed_ref, prob_ref, out_ref, padded):
    sources, streams, rows, _ = x_ref.shape
    tokens = sources * rows
    head = pl.program_id(0)
    lanes = pl.ds(pl.multiple_of(head * HEAD_DIM, HEAD_DIM), HEAD_DIM)
    padded[:, 0:PAD, :] = before_ref[:, :, lanes].astype(jnp.float32)
    for m in range(streams):
        padded[m, PAD:, :] = x_ref[:, m, :, lanes].reshape(tokens, HEAD_DIM).astype(jnp.float32)
    for m in range(streams):
        for start in range(0, tokens, BLOCK):
            total = None
            for lag in range(KW):
                at = PAD + start - lag
                term = taps_ref[m, lag : lag + 1, lanes] * padded[m, at : at + BLOCK, :]
                total = term if total is None else total + term
            mixed_ref[0, m, start : start + BLOCK, :] = total.astype(jnp.bfloat16)
    below = lax.broadcasted_iota(jnp.int32, (BLOCK, BLOCK), 0) >= lax.broadcasted_iota(
        jnp.int32, (BLOCK, BLOCK), 1
    )
    starts = tile_starts(tokens)[0]
    for group, first in row_groups(tokens):
        own = slice(group[0] * BLOCK, (group[-1] + 1) * BLOCK)
        span = slice(first * BLOCK, own.stop)
        raw = dot(mixed_ref[0, 0, own, :], mixed_ref[0, 1, span, :], ((1,), (1,)))
        sheets, inverses = [], []
        for block in group:
            lowest = max(0, block - STEPS)
            mine = raw[(block - group[0]) * BLOCK : (block - group[0] + 1) * BLOCK]
            parts = []
            for other in range(lowest, block + 1):
                part = mine[:, (other - first) * BLOCK : (other - first + 1) * BLOCK]
                allowed = below if other == block else docs[other] == docs[block]
                parts.append(jnp.where(allowed, part, -1e30))
            masked = jnp.concatenate(parts, axis=1) if len(parts) > 1 else parts[0]
            expo = jnp.exp2((masked - jnp.max(masked, axis=1, keepdims=True)) * SCALE_LOG2)
            inverses.append(1.0 / jnp.sum(expo, axis=1, keepdims=True))
            sheets.append(widened(expo.astype(jnp.bfloat16), block, group, first))
            prob = expo * inverses[-1]
            for n in range(block + 1 - lowest):
                prob_ref[0, starts[block] + n] = prob[:, n * BLOCK : (n + 1) * BLOCK]
        total = dot(stacked(sheets), mixed_ref[0, 2, span, :], ((1,), (0,)))
        per = out_ref.shape[1]
        for n, block in enumerate(group):
            at = block * BLOCK
            out_ref[at // per, at % per : at % per + BLOCK, :] = (
                total[n * BLOCK : (n + 1) * BLOCK] * inverses[n]
            ).astype(jnp.bfloat16)


def forward(docs, x, taps, before, members):
    sources, streams, rows, width = x.shape
    per = width // HEAD_DIM
    tokens = sources * rows
    tiles = tile_starts(tokens)[1]
    here = pl.BlockSpec(memory_space=pltpu.VMEM)
    return pl.pallas_call(
        forward_kernel,
        grid_spec=pltpu.PrefetchScalarGridSpec(
            num_scalar_prefetch=1,
            grid=(per,),
            in_specs=[here, here, here],
            out_specs=[
                pl.BlockSpec((1, streams, tokens, HEAD_DIM), lambda h, d: (h, 0, 0, 0)),
                pl.BlockSpec((1, tiles, BLOCK, BLOCK), lambda h, d: (h, 0, 0, 0)),
                pl.BlockSpec((members, tokens // members, HEAD_DIM), lambda h, d: (0, 0, h)),
            ],
            scratch_shapes=[pltpu.VMEM((streams, tokens + PAD, HEAD_DIM), jnp.float32)],
        ),
        out_shape=[
            pltpu.HBM((per, streams, tokens, HEAD_DIM), jnp.bfloat16),
            pltpu.HBM((per, tiles, BLOCK, BLOCK), jnp.float32),
            pltpu.HBM((members, tokens // members, width), jnp.bfloat16),
        ],
        compiler_params=room(FORE),
        cost_estimate=estimate(10_000_000_000, 8 * x.size),
        name="forward",
    )(docs, x, taps, before)


def backward_kernel(
    local, x_ref, before_ref, mixed_ref, prob_ref, att_ref, *refs
):
    *up_refs, cgrad_ref, tapg_ref, head_ref, up_ref = refs
    sources, streams, rows, _ = x_ref.shape
    tokens = sources * rows
    per = att_ref.shape[1]
    head = pl.program_id(0)

    @pl.when(head == 0)
    def _():
        for step, piece_ref in enumerate(up_refs):
            up_ref[local[0] ^ step] = piece_ref[...]

    lanes = pl.ds(pl.multiple_of(head * HEAD_DIM, HEAD_DIM), HEAD_DIM)
    cgrad = cgrad_ref.at[head]
    edge = jnp.zeros((streams, PAD, HEAD_DIM), jnp.float32)
    cgrad[:, 0:PAD, :] = edge
    cgrad[:, PAD + tokens :, :] = edge
    starts = tile_starts(tokens)[0]
    for group, first in row_groups(tokens):
        own = slice(group[0] * BLOCK, (group[-1] + 1) * BLOCK)
        span = slice(first * BLOCK, own.stop)
        query, keys = mixed_ref[0, 0, own, :], mixed_ref[0, 1, span, :]
        ups = [
            up_ref[b * BLOCK // per, b * BLOCK % per : b * BLOCK % per + BLOCK, lanes]
            for b in group
        ]
        up = stacked(ups)
        dprob = dot(up, mixed_ref[0, 2, span, :], ((1,), (1,)))
        probs, dscores = [], []
        for n, block in enumerate(group):
            lowest, at = max(0, block - STEPS), block * BLOCK
            att = att_ref[at // per, at % per : at % per + BLOCK, :]
            delta = jnp.sum(
                ups[n].astype(jnp.float32) * att.astype(jnp.float32), axis=1, keepdims=True
            )
            tiles = [prob_ref[0, starts[block] + k] for k in range(block + 1 - lowest)]
            prob = jnp.concatenate(tiles, axis=1) if len(tiles) > 1 else tiles[0]
            mine = dprob[
                n * BLOCK : (n + 1) * BLOCK,
                (lowest - first) * BLOCK : (block + 1 - first) * BLOCK,
            ]
            dscore = (prob * (mine - delta) * SCALE).astype(jnp.bfloat16)
            dscores.append(widened(dscore, block, group, first))
            probs.append(widened(prob.astype(jnp.bfloat16), block, group, first))
        dscore = stacked(dscores)
        out = slice(PAD + own.start, PAD + own.stop)
        outs = slice(PAD + span.start, PAD + own.start)
        cgrad[0, out, :] = dot(dscore, keys, ((1,), (0,)))
        for m, part in (
            (1, dot(dscore, query, ((0,), (0,)))),
            (2, dot(stacked(probs), up, ((0,), (0,)))),
        ):
            if span.start < own.start:
                cgrad[m, outs, :] += part[: own.start - span.start]
            cgrad[m, out, :] = part[own.start - span.start :]
    head_ref[:, :, lanes] = cgrad[:, PAD : 2 * PAD, :]
    span = BLOCK // rows
    for m in range(streams):
        early = before_ref[m, :, lanes].astype(jnp.float32)
        sums = [early * cgrad[m, lag : lag + PAD, :] for lag in range(KW)]
        for start in range(0, tokens, BLOCK):
            at = start // rows
            here = x_ref[at : at + span, m].reshape(BLOCK, HEAD_DIM).astype(jnp.float32)
            for lag in range(KW):
                product = here * cgrad[m, PAD + start + lag : PAD + start + lag + BLOCK, :]
                sums[lag] = sums[lag] + jnp.sum(product.reshape(BLOCK // 8, 8, HEAD_DIM), axis=0)
        for lag in range(KW):
            tapg_ref[m, lag : lag + 1, lanes] = jnp.sum(sums[lag], axis=0, keepdims=True)


def backward(local, x, before, mixed, prob, att, pieces):
    sources, streams, rows, width = x.shape
    per = width // HEAD_DIM
    tokens = sources * rows
    members = att.shape[0]
    tiles = prob.shape[1]
    here = pl.BlockSpec(memory_space=pltpu.VMEM)
    return pl.pallas_call(
        backward_kernel,
        grid_spec=pltpu.PrefetchScalarGridSpec(
            num_scalar_prefetch=1,
            grid=(per,),
            in_specs=[
                pl.BlockSpec((sources, streams, rows, HEAD_DIM), lambda h, p: (0, 0, 0, h)),
                here,
                pl.BlockSpec((1, streams, tokens, HEAD_DIM), lambda h, p: (h, 0, 0, 0)),
                pl.BlockSpec((1, tiles, BLOCK, BLOCK), lambda h, p: (h, 0, 0, 0)),
                pl.BlockSpec((members, tokens // members, HEAD_DIM), lambda h, p: (0, 0, h)),
            ]
            + [here] * members,
            out_specs=[here, here, here],
            scratch_shapes=[pltpu.VMEM((members, tokens // members, width), jnp.bfloat16)],
        ),
        out_shape=[
            jax.ShapeDtypeStruct((per, streams, tokens + 2 * PAD, HEAD_DIM), jnp.float32),
            jax.ShapeDtypeStruct((streams, KW, width), jnp.float32),
            jax.ShapeDtypeStruct((streams, PAD, width), jnp.float32),
        ],
        compiler_params=room(BACK),
        cost_estimate=estimate(20_000_000_000, 12 * x.size),
        name="backward",
    )(local, x, before, mixed, prob, att, *pieces)


def spread_kernel(cgrad_ref, taps_ref, grad_ref, tail_ref):
    _, streams, rows, _ = grad_ref.shape
    head = pl.program_id(0)
    lanes = pl.ds(pl.multiple_of(head * HEAD_DIM, HEAD_DIM), HEAD_DIM)
    for m in range(streams):
        for start in range(0, cgrad_ref.shape[2] - 2 * PAD, BLOCK):
            total = None
            for lag in range(KW):
                at = PAD + start + lag
                term = taps_ref[m, lag : lag + 1, lanes] * cgrad_ref[head, m, at : at + BLOCK, :]
                total = term if total is None else total + term
            grad_ref[start // rows : (start + BLOCK) // rows, m] = total.astype(
                jnp.bfloat16
            ).reshape(BLOCK // rows, rows, HEAD_DIM)
        tail_ref[m, :, lanes] = total[BLOCK - PAD :]


def spread(cgrad, taps, rows):
    per, streams, longer, _ = cgrad.shape
    sources, width = (longer - 2 * PAD) // rows, per * HEAD_DIM
    here = pl.BlockSpec(memory_space=pltpu.VMEM)
    return pl.pallas_call(
        spread_kernel,
        grid=(per,),
        in_specs=[here, here],
        out_specs=[
            pl.BlockSpec((sources, streams, rows, HEAD_DIM), lambda h: (0, 0, 0, h)),
            here,
        ],
        out_shape=[
            pltpu.HBM((sources, streams, rows, width), jnp.bfloat16),
            jax.ShapeDtypeStruct((streams, PAD, width), jnp.float32),
        ],
        compiler_params=room(SPREAD),
        cost_estimate=estimate(2_000_000_000, 6 * cgrad.size),
        name="spread",
    )(cgrad, taps)


def swap(value, axes, groups):
    shape = value.shape
    return lax.all_to_all(
        value.reshape(shape[0], -1, shape[-1]),
        axes,
        split_axis=0,
        concat_axis=0,
        axis_index_groups=groups,
        tiled=True,
    ).reshape(shape)


def across(value, step):
    count = lax.axis_size("ctx")
    return lax.ppermute(value, "ctx", [(i, i ^ step) for i in range(count)])


def first_exchange(piece, members):
    if members < lax.axis_size("ctx"):
        return 1, piece + across(piece, members)
    other = across(piece, 1)
    even = lax.axis_index("ctx") % 2 == 0
    return 2, jnp.concatenate(
        [jnp.where(even, piece, other), jnp.where(even, other, piece)], axis=-1
    )


def gather_columns(held, span, members):
    position = lax.axis_index("ctx").astype(jnp.int32)
    streams, taps, wide = held.shape
    steps = range(0, members, span)
    pieces = [across(held, step) if step else held for step in steps]

    def kernel(position_ref, *refs):
        o_ref = refs[-1]
        for step in steps:
            column = lax.rem(position_ref[0] ^ step, members) // span
            o_ref[:, :, pl.ds(pl.multiple_of(column * wide, wide), wide)] = refs[step // span][...]

    columns = members // span * wide
    return pl.pallas_call(
        kernel,
        grid_spec=pltpu.PrefetchScalarGridSpec(
            num_scalar_prefetch=1,
            grid=(1,),
            in_specs=[pl.BlockSpec((streams, taps, wide), lambda i, p: (0, 0, 0))] * len(pieces),
            out_specs=pl.BlockSpec((streams, taps, columns), lambda i, p: (0, 0, 0)),
        ),
        out_shape=jax.ShapeDtypeStruct((streams, taps, columns), held.dtype),
        compiler_params=room(4),
        name="place_columns",
    )(position.reshape(1), *pieces)


def by_heads(parts, qkv, filters, doc_ids, upstream):
    count, tp = lax.axis_size("ctx"), lax.axis_size("tp")
    members = count // parts
    rows, streams, _ = qkv.shape
    width = upstream.shape[1] // members
    position = lax.axis_index("ctx")
    every = everywhere = None
    if parts > 1:
        every = [[p * members + c for c in range(members)] for p in range(parts)]
        everywhere = [[c * tp + t for c in group for t in range(tp)] for group in every]
        blocks = doc_ids.shape[0] // parts
        doc_ids = lax.dynamic_slice_in_dim(doc_ids, position // members * blocks, blocks)
    slabs = split_columns(jnp.transpose(qkv, (1, 0, 2)), members, tp, 60)
    x = swap(slabs.reshape((members * tp,) + slabs.shape[2:]), AXES, everywhere)
    local = (position % members).astype(jnp.int32).reshape(1)
    pieces = split_rows(upstream, members, local)
    pieces = [across(piece, step) if step else piece for step, piece in enumerate(pieces)]
    taps = lax.dynamic_slice_in_dim(filters, position % members * width, width, 2)
    if parts > 1:
        upward = [(i, i + members) for i in range(count - members)]
        before = lax.ppermute(x[-1, :, rows - PAD :], "ctx", upward)
    else:
        before = jnp.zeros((streams, PAD, width), x.dtype)
    mixed, prob, att = forward(doc_ids, x, taps, before, members)
    attended = join_columns(swap(att, "ctx", every)[:, None, None])[0]
    away = [pltpu.with_memory_space_constraint(v, pltpu.HBM) for v in (mixed, prob, att)]
    cgrad, tap_grad, head = backward(local, x, before, *away, pieces)
    span, held = first_exchange(tap_grad, members)
    grad, tail = spread(cgrad, taps, rows)
    if parts > 1:
        after = lax.ppermute(head, "ctx", [(to, source) for source, to in upward])
        after = jnp.concatenate([jnp.zeros_like(after), after], axis=1)
        for lag in range(KW):
            tail = tail + taps[:, lag : lag + 1] * after[:, lag : lag + PAD]
        grad = grad.at[-1, :, rows - PAD :].set(tail.astype(grad.dtype))
    grad, held = lax.optimization_barrier((grad, held))
    held, attended = lax.optimization_barrier((held, attended))
    filter_grad = gather_columns(held, span, members)
    qkv_grad = join_columns(swap(grad, AXES, everywhere).reshape(slabs.shape))
    return attended, jnp.transpose(qkv_grad, (1, 0, 2)), filter_grad


def from_behind(value, axis, steps):
    count = lax.axis_size(axis)
    first, last = (max(0, -steps), min(count, count - steps))
    return lax.ppermute(value, axis, [(source, source + steps) for source in range(first, last)])


def block_docs(doc_ids, first_block, count):
    start = jnp.maximum(first_block, 0)
    picked = lax.dynamic_slice_in_dim(doc_ids, start, count)
    return jnp.repeat(picked, BLOCK)


def by_ring(qkv, filters, doc_ids, upstream):
    local = lax.all_to_all(qkv, "tp", split_axis=2, concat_axis=0, tiled=True)
    tokens = local.shape[0]
    width = local.shape[2]
    heads = width // HEAD_DIM
    blocks_here = tokens // BLOCK
    logit_scale = HEAD_DIM ** (-0.5)
    position = lax.axis_index("ctx")
    reach = STEPS + 1
    rim = from_behind(local[tokens - (KW - 1) :], "ctx", 1)
    inputs = jnp.concatenate([rim, local], axis=0).astype(jnp.float32)
    mixed = sum(
        (filters[:, lag, :] * inputs[KW - 1 - lag : KW - 1 - lag + tokens] for lag in range(KW))
    )
    mixed = mixed.astype(jnp.bfloat16)
    queries = mixed[:, 0].reshape(tokens, heads, HEAD_DIM)
    key_value = mixed[:, 1:3]
    tiles = [key_value]
    current = key_value
    for distance in range(1, STEPS + 1):
        current = from_behind(current, "ctx", 1)
        tiles.append(current)
    joined = jnp.concatenate(tiles, axis=0)
    keys = joined[:, 0].reshape(reach * tokens, heads, HEAD_DIM)
    values = joined[:, 1].reshape(reach * tokens, heads, HEAD_DIM)
    rows = jnp.arange(tokens)
    query_token = position * tokens + rows
    query_doc = block_docs(doc_ids, position * blocks_here, blocks_here)
    key_tokens = jnp.concatenate(
        [(position - distance) * tokens + rows for distance in range(reach)]
    )
    key_docs = jnp.concatenate(
        [
            block_docs(doc_ids, (position - distance) * blocks_here, blocks_here)
            for distance in range(reach)
        ]
    )
    allowed = (
        (key_tokens[None, :] >= 0)
        & (key_tokens[None, :] <= query_token[:, None])
        & (key_docs[None, :] == query_doc[:, None])
    )
    raw = (
        jnp.einsum("qhd,khd->hqk", queries, keys, preferred_element_type=jnp.float32) * logit_scale
    )
    masked = jnp.where(allowed[None], raw, -1e30)
    row_max = masked.max(axis=2)
    expo = jnp.where(allowed[None], jnp.exp(masked - row_max[:, :, None]), 0.0)
    row_sum = expo.sum(axis=2)
    weighted_values = jnp.einsum(
        "hqk,khd->qhd", expo.astype(jnp.bfloat16), values, preferred_element_type=jnp.float32
    )
    attended = (weighted_values / row_sum.T[:, :, None]).astype(jnp.bfloat16)
    grad_out = upstream.reshape(tokens, heads, HEAD_DIM)
    delta = jnp.sum(grad_out.astype(jnp.float32) * attended.astype(jnp.float32), axis=-1).T
    prob = expo / row_sum[:, :, None]
    value_part = jnp.einsum(
        "hqk,qhd->khd", prob.astype(jnp.bfloat16), grad_out, preferred_element_type=jnp.float32
    )
    probability_gradient = jnp.einsum(
        "qhd,khd->hqk", grad_out, values, preferred_element_type=jnp.float32
    )
    score_gradient = (prob * (probability_gradient - delta[:, :, None]) * logit_scale).astype(
        jnp.bfloat16
    )
    query_gradient_rows = jnp.einsum(
        "hqk,khd->qhd", score_gradient, keys, preferred_element_type=jnp.float32
    )
    key_part = jnp.einsum(
        "hqk,qhd->khd", score_gradient, queries, preferred_element_type=jnp.float32
    )
    stacked = jnp.stack(
        [key_part.reshape(reach, tokens, width), value_part.reshape(reach, tokens, width)], axis=2
    )
    partials = [stacked[distance] for distance in range(reach)]
    carried = partials[STEPS]
    for distance in range(STEPS - 1, -1, -1):
        carried = from_behind(carried, "ctx", -1)
        carried = carried + partials[distance]
    conv_grad = jnp.concatenate([query_gradient_rows.reshape(tokens, 1, width), carried], axis=1)
    grad_edge = from_behind(conv_grad[: KW - 1], "ctx", -1)
    extended = jnp.concatenate([conv_grad, grad_edge], axis=0)
    input_grad = sum((filters[:, lag, :] * extended[lag : lag + tokens] for lag in range(KW)))
    tap_terms = jnp.stack(
        [
            jnp.sum(inputs[KW - 1 - lag : KW - 1 - lag + tokens] * conv_grad, axis=0)
            for lag in range(KW)
        ],
        axis=1,
    )
    filter_grad = lax.psum(tap_terms, "ctx")
    qkv_grad = lax.all_to_all(
        input_grad.astype(jnp.bfloat16), "tp", split_axis=0, concat_axis=2, tiled=True
    )
    return (attended.reshape(tokens, width), qkv_grad, filter_grad)


def solution(mesh):
    count = mesh.shape["ctx"]

    def shards(qkv, filters, doc_ids, upstream):
        tokens, width = upstream.shape
        heads = width // HEAD_DIM
        args = (qkv, filters, doc_ids, upstream)
        even = tokens % BLOCK == 0 and qkv.shape[0] % PAD == 0 and count & (count - 1) == 0
        if heads % count or not even or count < 4:
            return by_ring(*args)
        middle = doc_ids.shape[0] // 2
        apart = doc_ids[middle - 1] != doc_ids[middle]
        return lax.cond(
            apart, functools.partial(by_heads, 2), functools.partial(by_heads, 1), *args
        )

    return jax.shard_map(
        shards,
        mesh=mesh,
        in_specs=(P(("ctx", "tp"), None, None), P(None, None, "tp"), P(), P("ctx", "tp")),
        out_specs=(P("ctx", "tp"), P(("ctx", "tp"), None, None), P(None, None, "tp")),
        check_vma=False,
    )
```

profile of v0, /device:TPU:0, one launch (start us, length us, event | category | flops | bytes accessed | tf_op | source)
XLA Modules:
  0.0 128.5 jit_solution(9874842261959054782)
XLA Ops:
  0.6 1.3 %fusion.13 = (s32[1]{0:T(128)}, s32[1]{0:T(128)}) fusion(s32[8]{0:T(128)} %param.10), kind=kLoop, calls=%fused_computation.40 | loop fusion | bytes 16 | tf_op jit(solution)/shard_map/slice | solution.py:575
  3.2 125.2 %conditional.1 = (bf16[128,2048]{1,0:T(8,128)(2,1)}, bf16[32,3,8192]{2,0,1:T(8,128)(2,1)}, f32[3,7,2048]{2,1,0:T(8,128)}) conditional(s32[]{:T(128)} %bitcast.22, (bf16[32,3,8192]{2,0,1:T(8,128)(2,1)}, f32[3,7,2048]{2,1,0:T(8,128)}, s32[8]{0:T(128)}, bf16[128,2048]{1,0:T(8,128)(2,1)}) %tuple.23, (bf16[32,3,8192]{2,0,1:T(8,128)(2,1)}, s32[8]{0:T(128)}, ...), branch_computations={%region_0.1_spmd, %region_1.2_spmd} | conditional | flops 32000184320 | bytes 45249628 | solution.py:576
  3.3 2.3 %split_columns.2 = bf16[8,4,3,32,256]{4,3,2,1,0:T(8,128)(2,1)} custom-call(bf16[3,32,8192]{2,1,0:T(8,128)(2,1)} %bitcast.49), custom_call_target="tpu_custom_call" | custom-call | bytes 3145728 | tf_op jit(solution)/shard_map/cond/branch_0_fun/split_columns/pallas_call | solution.py:46
  5.6 0.0 copy-start
  5.6 0.0 copy-start.2
  5.6 7.3 %all-to-all-start = ((bf16[32,96,256]{2,1,0:T(8,128)(2,1)}), bf16[32,96,256]{2,1,0:T(8,128)(2,1)S(1)}, u32[]{:S(2)}, u32[]{:S(2)}) async-start(bf16[32,96,256]{2,1,0:T(8,128)(2,1)} %bitcast.51), calls=%async_computation | async-start | bytes 3145728 | tf_op jit(solution)/shard_map/cond/branch_0_fun/all_to_all | solution.py:361
  12.9 0.0 copy-done
  12.9 0.1 split_rows.2
  13.0 1.8 %collective-permute-start = (bf16[128,256]{1,0:T(8,128)(2,1)S(1)}, bf16[128,256]{1,0:T(8,128)(2,1)S(1)}, u32[]{:S(2)}, u32[]{:S(2)}) collective-permute-start(bf16[128,256]{1,0:T(8,128)(2,1)S(1)} %get-tuple-element.36), channel_id=1, source_target_pairs={{0,4},{4,0},{8,12},{12,8},{16,20},{20,16},{24,28},{28,24},{1,5},{5... | collective-permute-start | bytes 196616 | tf_op jit(solution)/shard_map/cond/branch_0_fun/ppermute | solution.py:373
  14.8 1.5 %collective-permute-start.1 = (bf16[128,256]{1,0:T(8,128)(2,1)S(1)}, bf16[128,256]{1,0:T(8,128)(2,1)S(1)}, u32[]{:S(2)}, u32[]{:S(2)}) collective-permute-start(bf16[128,256]{1,0:T(8,128)(2,1)S(1)} %get-tuple-element.37), channel_id=1, source_target_pairs={{0,8},{4,12},{8,0},{12,4},{16,24},{20,28},{24,16},{28,20},{1,9},{5... | collective-permute-start | bytes 196616 | tf_op jit(solution)/shard_map/cond/branch_0_fun/ppermute | solution.py:373
  16.3 0.3 collective-permute-start.2
  16.6 2.7 %collective-permute-start.3 = (bf16[128,256]{1,0:T(8,128)(2,1)S(1)}, bf16[128,256]{1,0:T(8,128)(2,1)S(1)}, u32[]{:S(2)}, u32[]{:S(2)}) collective-permute-start(bf16[128,256]{1,0:T(8,128)(2,1)S(1)} %get-tuple-element.39), channel_id=1, source_target_pairs={{0,16},{4,20},{8,24},{12,28},{16,0},{20,4},{24,8},{28,12},{1,17},{... | collective-permute-start | bytes 196616 | tf_op jit(solution)/shard_map/cond/branch_0_fun/ppermute | solution.py:373
  19.2 1.5 %collective-permute-start.4 = (bf16[128,256]{1,0:T(8,128)(2,1)S(1)}, bf16[128,256]{1,0:T(8,128)(2,1)S(1)}, u32[]{:S(2)}, u32[]{:S(2)}) collective-permute-start(bf16[128,256]{1,0:T(8,128)(2,1)S(1)} %get-tuple-element.40), channel_id=1, source_target_pairs={{0,20},{4,16},{8,28},{12,24},{16,4},{20,0},{24,12},{28,8},{1,21},{... | collective-permute-start | bytes 196616 | tf_op jit(solution)/shard_map/cond/branch_0_fun/ppermute | solution.py:373
  20.7 0.7 constant_dynamic-slice_fusion.taps_ref
  21.4 1.5 %collective-permute-done.refs_1_ = bf16[128,256]{1,0:T(8,128)(2,1)S(1)} collective-permute-done((bf16[128,256]{1,0:T(8,128)(2,1)S(1)}, bf16[128,256]{1,0:T(8,128)(2,1)S(1)}, u32[]{:S(2)}, u32[]{:S(2)}) %collective-permute-start) | collective-permute-done | bytes 65568 | tf_op jit(solution)/shard_map/cond/branch_0_fun/ppermute | solution.py:373
  22.9 5.7 %collective-permute-start.5 = (bf16[128,256]{1,0:T(8,128)(2,1)S(1)}, bf16[128,256]{1,0:T(8,128)(2,1)S(1)}, u32[]{:S(2)}, u32[]{:S(2)}) collective-permute-start(bf16[128,256]{1,0:T(8,128)(2,1)S(1)} %get-tuple-element.41), channel_id=1, source_target_pairs={{0,24},{4,28},{8,16},{12,20},{16,8},{20,12},{24,0},{28,4},{1,25},{... | collective-permute-start | bytes 196616 | tf_op jit(solution)/shard_map/cond/branch_0_fun/ppermute | solution.py:373
  28.7 12.3 %collective-permute-done.1.refs_2_ = bf16[128,256]{1,0:T(8,128)(2,1)S(1)} collective-permute-done((bf16[128,256]{1,0:T(8,128)(2,1)S(1)}, bf16[128,256]{1,0:T(8,128)(2,1)S(1)}, u32[]{:S(2)}, u32[]{:S(2)}) %collective-permute-start.1) | collective-permute-done | bytes 65568 | tf_op jit(solution)/shard_map/cond/branch_0_fun/ppermute | solution.py:373
  41.0 4.4 %collective-permute-start.6 = (bf16[128,256]{1,0:T(8,128)(2,1)S(1)}, bf16[128,256]{1,0:T(8,128)(2,1)S(1)}, u32[]{:S(2)}, u32[]{:S(2)}) collective-permute-start(bf16[128,256]{1,0:T(8,128)(2,1)S(1)} %get-tuple-element.42), channel_id=1, source_target_pairs={{0,28},{4,24},{8,20},{12,16},{16,12},{20,8},{24,4},{28,0},{1,29},{... | collective-permute-start | bytes 196616 | tf_op jit(solution)/shard_map/cond/branch_0_fun/ppermute | solution.py:373
  45.4 11.3 %all-to-all-done = bf16[32,96,256]{2,1,0:T(8,128)(2,1)S(1)} async-done(((bf16[32,96,256]{2,1,0:T(8,128)(2,1)}), bf16[32,96,256]{2,1,0:T(8,128)(2,1)S(1)}, u32[]{:S(2)}, u32[]{:S(2)}) %all-to-all-start) | async-done | bytes 1572896 | tf_op jit(solution)/shard_map/cond/branch_0_fun/all_to_all | solution.py:361
  56.7 0.0 copy-done.2
  56.7 6.2 %forward.2 = (bf16[2,3,1024,128]{3,2,1,0:T(8,128)(2,1)}, f32[2,30,128,128]{3,2,1,0:T(8,128)}, bf16[8,128,256]{2,1,0:T(8,128)(2,1)}) custom-call(s32[8]{0:T(128)S(1)} %copy-done.2, bf16[32,3,32,256]{3,2,1,0:T(8,128)(2,1)S(1)} %bitcast.47, f32[3,7,256]{2,1,0:T(8,128)S(1)} %constant_dynamic-slice_fusion.taps_ref, ...), custom_call_target="tpu_custom_call" | custom-call | flops 10000000000 | bytes 6291456 | tf_op jit(solution)/shard_map/cond/branch_0_fun/forward/pallas_call | solution.py:190
  62.9 3.5 %all-to-all-start.1 = ((bf16[8,128,256]{2,1,0:T(8,128)(2,1)}), bf16[8,128,256]{2,1,0:T(8,128)(2,1)S(1)}, u32[]{:S(2)}, u32[]{:S(2)}) async-start(bf16[8,128,256]{2,1,0:T(8,128)(2,1)} %get-tuple-element.33.att_ref), calls=%async_computation.1 | async-start | bytes 1048576 | tf_op jit(solution)/shard_map/cond/branch_0_fun/all_to_all | solution.py:361
  66.4 0.0 collective-permute-done.2.refs_3_
  66.4 0.0 collective-permute-done.3.refs_4_
  66.5 0.0 collective-permute-done.4.refs_5_
  66.5 0.0 collective-permute-done.5.refs_6_
  66.5 0.0 collective-permute-done.6.refs_7_
  66.5 6.6 %backward.2 = (f32[2,3,1040,128]{3,2,1,0:T(8,128)S(1)}, f32[3,7,256]{2,1,0:T(8,128)S(1)}, f32[3,8,256]{2,1,0:T(8,128)}) custom-call(s32[1]{0:T(128)} %bitcast.local_ref.local, bf16[32,3,32,256]{3,2,1,0:T(8,128)(2,1)S(1)} %bitcast.48, bf16[3,8,256]{2,1,0:T(8,128)(2,1)S(1)} %broadcast_1_before_ref.0.before_ref, ...), custom_call_target="tpu_custom_call" | custom-call | flops 20000000000 | bytes 9437184 | tf_op jit(solution)/shard_map/cond/branch_0_fun/backward/pallas_call | solution.py:293
  73.0 2.0 %collective-permute-start.7 = (f32[3,7,256]{2,1,0:T(8,128)S(1)}, f32[3,7,256]{2,1,0:T(8,128)S(1)}, u32[]{:S(2)}, u32[]{:S(2)}) collective-permute-start(f32[3,7,256]{2,1,0:T(8,128)S(1)} %get-tuple-element.45), channel_id=1, source_target_pairs={{0,4},{4,0},{8,12},{12,8},{16,20},{20,16},{24,28},{28,24},{1,5},{5... | collective-permute-start | bytes 64520 | tf_op jit(solution)/shard_map/cond/branch_0_fun/ppermute | solution.py:373
  75.0 2.3 %spread.2 = (bf16[32,3,32,256]{3,2,1,0:T(8,128)(2,1)}, f32[3,8,256]{2,1,0:T(8,128)}) custom-call(f32[2,3,1040,128]{3,2,1,0:T(8,128)S(1)} %get-tuple-element.43.cgrad_ref, f32[3,7,256]{2,1,0:T(8,128)S(1)} %constant_dynamic-slice_fusion.taps_ref), custom_call_target="tpu_custom_call" | custom-call | flops 2000000000 | bytes 4792320 | tf_op jit(solution)/shard_map/cond/branch_0_fun/spread/pallas_call | solution.py:341
  77.3 0.0 collective-permute-done.7
  77.4 3.3 %all-to-all-done.1 = bf16[8,128,256]{2,1,0:T(8,128)(2,1)S(1)} async-done(((bf16[8,128,256]{2,1,0:T(8,128)(2,1)}), bf16[8,128,256]{2,1,0:T(8,128)(2,1)S(1)}, u32[]{:S(2)}, u32[]{:S(2)}) %all-to-all-start.1) | async-done | bytes 524320 | tf_op jit(solution)/shard_map/cond/branch_0_fun/all_to_all | solution.py:361
  80.6 4.0 %all-to-all-start.2 = ((bf16[32,96,256]{2,1,0:T(8,128)(2,1)}), bf16[32,96,256]{2,1,0:T(8,128)(2,1)S(1)}, u32[]{:S(2)}, u32[]{:S(2)}) async-start(bf16[32,96,256]{2,1,0:T(8,128)(2,1)} %bitcast.53), calls=%async_computation.2 | async-start | bytes 3145728 | tf_op jit(solution)/shard_map/cond/branch_0_fun/all_to_all | solution.py:361
  84.6 0.8 join_columns.4
  85.4 3.6 %collective-permute-start.10 = (f32[3,7,512]{2,1,0:T(8,128)S(1)}, f32[3,7,512]{2,1,0:T(8,128)S(1)}, u32[]{:S(2)}, u32[]{:S(2)}) collective-permute-start(f32[3,7,512]{2,1,0:T(8,128)S(1)} %pad_maximum_fusion.refs_0_), channel_id=1, source_target_pairs={{0,24},{4,28},{8,16},{12,20},{16,8},{20,12},{24,0},{28,4},{1,25},{... | collective-permute-start | bytes 129032 | tf_op jit(solution)/shard_map/cond/branch_0_fun/ppermute | solution.py:373
  89.1 0.0 collective-permute-start.9
  89.1 0.8 collective-permute-start.8
  89.8 26.3 %collective-permute-done.10.refs_3_ = f32[3,7,512]{2,1,0:T(8,128)S(1)} collective-permute-done((f32[3,7,512]{2,1,0:T(8,128)S(1)}, f32[3,7,512]{2,1,0:T(8,128)S(1)}, u32[]{:S(2)}, u32[]{:S(2)}) %collective-permute-start.10) | collective-permute-done | bytes 43040 | tf_op jit(solution)/shard_map/cond/branch_0_fun/ppermute | solution.py:373
  116.2 10.4 %collective-permute-done.9.refs_2_ = f32[3,7,512]{2,1,0:T(8,128)S(1)} collective-permute-done((f32[3,7,512]{2,1,0:T(8,128)S(1)}, f32[3,7,512]{2,1,0:T(8,128)S(1)}, u32[]{:S(2)}, u32[]{:S(2)}) %collective-permute-start.9) | collective-permute-done | bytes 43040 | tf_op jit(solution)/shard_map/cond/branch_0_fun/ppermute | solution.py:373
  126.5 0.0 collective-permute-done.8.refs_1_
  126.5 0.7 place_columns.2
  127.2 0.0 all-to-all-done.2
  127.2 1.2 join_columns.5
  (3 shorter events, 0.0 us)
Async XLA Ops:
  5.6 7.3 %copy-start = (bf16[128,2048]{1,0:T(8,128)(2,1)S(1)}, bf16[128,2048]{1,0:T(8,128)(2,1)}, u32[]{:S(2)}) copy-start(bf16[128,2048]{1,0:T(8,128)(2,1)} %get-tuple-element.34.x_ref) | copy-start | bytes 1572868 | tf_op jit(solution)/shard_map/cond
  5.6 51.1 %copy-start.2 = (s32[8]{0:T(128)S(1)}, s32[8]{0:T(128)}, u32[]{:S(2)}) copy-start(s32[8]{0:T(128)} %get-tuple-element.29.docs) | copy-start | bytes 100 | tf_op jit(solution)/shard_map/cond
  5.6 51.1 %all-to-all-start = ((bf16[32,96,256]{2,1,0:T(8,128)(2,1)}), bf16[32,96,256]{2,1,0:T(8,128)(2,1)S(1)}, u32[]{:S(2)}, u32[]{:S(2)}) async-start(bf16[32,96,256]{2,1,0:T(8,128)(2,1)} %bitcast.51), calls=%async_computation | async-start | bytes 3145728 | tf_op jit(solution)/shard_map/cond/branch_0_fun/all_to_all | solution.py:361
  13.0 9.9 %collective-permute-start = (bf16[128,256]{1,0:T(8,128)(2,1)S(1)}, bf16[128,256]{1,0:T(8,128)(2,1)S(1)}, u32[]{:S(2)}, u32[]{:S(2)}) collective-permute-start(bf16[128,256]{1,0:T(8,128)(2,1)S(1)} %get-tuple-element.36), channel_id=1, source_target_pairs={{0,4},{4,0},{8,12},{12,8},{16,20},{20,16},{24,28},{28,24},{1,5},{5... | collective-permute-start | bytes 196616 | tf_op jit(solution)/shard_map/cond/branch_0_fun/ppermute | solution.py:373
  14.8 26.2 %collective-permute-start.1 = (bf16[128,256]{1,0:T(8,128)(2,1)S(1)}, bf16[128,256]{1,0:T(8,128)(2,1)S(1)}, u32[]{:S(2)}, u32[]{:S(2)}) collective-permute-start(bf16[128,256]{1,0:T(8,128)(2,1)S(1)} %get-tuple-element.37), channel_id=1, source_target_pairs={{0,8},{4,12},{8,0},{12,4},{16,24},{20,28},{24,16},{28,20},{1,9},{5... | collective-permute-start | bytes 196616 | tf_op jit(solution)/shard_map/cond/branch_0_fun/ppermute | solution.py:373
  16.3 50.1 %collective-permute-start.2 = (bf16[128,256]{1,0:T(8,128)(2,1)S(1)}, bf16[128,256]{1,0:T(8,128)(2,1)S(1)}, u32[]{:S(2)}, u32[]{:S(2)}) collective-permute-start(bf16[128,256]{1,0:T(8,128)(2,1)S(1)} %get-tuple-element.38), channel_id=1, source_target_pairs={{0,12},{4,8},{8,4},{12,0},{16,28},{20,24},{24,20},{28,16},{1,13},{... | collective-permute-start | bytes 196616 | tf_op jit(solution)/shard_map/cond/branch_0_fun/ppermute | solution.py:373
  16.6 49.9 %collective-permute-start.3 = (bf16[128,256]{1,0:T(8,128)(2,1)S(1)}, bf16[128,256]{1,0:T(8,128)(2,1)S(1)}, u32[]{:S(2)}, u32[]{:S(2)}) collective-permute-start(bf16[128,256]{1,0:T(8,128)(2,1)S(1)} %get-tuple-element.39), channel_id=1, source_target_pairs={{0,16},{4,20},{8,24},{12,28},{16,0},{20,4},{24,8},{28,12},{1,17},{... | collective-permute-start | bytes 196616 | tf_op jit(solution)/shard_map/cond/branch_0_fun/ppermute | solution.py:373
  19.2 47.2 %collective-permute-start.4 = (bf16[128,256]{1,0:T(8,128)(2,1)S(1)}, bf16[128,256]{1,0:T(8,128)(2,1)S(1)}, u32[]{:S(2)}, u32[]{:S(2)}) collective-permute-start(bf16[128,256]{1,0:T(8,128)(2,1)S(1)} %get-tuple-element.40), channel_id=1, source_target_pairs={{0,20},{4,16},{8,28},{12,24},{16,4},{20,0},{24,12},{28,8},{1,21},{... | collective-permute-start | bytes 196616 | tf_op jit(solution)/shard_map/cond/branch_0_fun/ppermute | solution.py:373
  22.9 43.5 %collective-permute-start.5 = (bf16[128,256]{1,0:T(8,128)(2,1)S(1)}, bf16[128,256]{1,0:T(8,128)(2,1)S(1)}, u32[]{:S(2)}, u32[]{:S(2)}) collective-permute-start(bf16[128,256]{1,0:T(8,128)(2,1)S(1)} %get-tuple-element.41), channel_id=1, source_target_pairs={{0,24},{4,28},{8,16},{12,20},{16,8},{20,12},{24,0},{28,4},{1,25},{... | collective-permute-start | bytes 196616 | tf_op jit(solution)/shard_map/cond/branch_0_fun/ppermute | solution.py:373
  41.0 25.5 %collective-permute-start.6 = (bf16[128,256]{1,0:T(8,128)(2,1)S(1)}, bf16[128,256]{1,0:T(8,128)(2,1)S(1)}, u32[]{:S(2)}, u32[]{:S(2)}) collective-permute-start(bf16[128,256]{1,0:T(8,128)(2,1)S(1)} %get-tuple-element.42), channel_id=1, source_target_pairs={{0,28},{4,24},{8,20},{12,16},{16,12},{20,8},{24,4},{28,0},{1,29},{... | collective-permute-start | bytes 196616 | tf_op jit(solution)/shard_map/cond/branch_0_fun/ppermute | solution.py:373
  62.9 17.7 %all-to-all-start.1 = ((bf16[8,128,256]{2,1,0:T(8,128)(2,1)}), bf16[8,128,256]{2,1,0:T(8,128)(2,1)S(1)}, u32[]{:S(2)}, u32[]{:S(2)}) async-start(bf16[8,128,256]{2,1,0:T(8,128)(2,1)} %get-tuple-element.33.att_ref), calls=%async_computation.1 | async-start | bytes 1048576 | tf_op jit(solution)/shard_map/cond/branch_0_fun/all_to_all | solution.py:361
  73.0 4.3 %collective-permute-start.7 = (f32[3,7,256]{2,1,0:T(8,128)S(1)}, f32[3,7,256]{2,1,0:T(8,128)S(1)}, u32[]{:S(2)}, u32[]{:S(2)}) collective-permute-start(f32[3,7,256]{2,1,0:T(8,128)S(1)} %get-tuple-element.45), channel_id=1, source_target_pairs={{0,4},{4,0},{8,12},{12,8},{16,20},{20,16},{24,28},{28,24},{1,5},{5... | collective-permute-start | bytes 64520 | tf_op jit(solution)/shard_map/cond/branch_0_fun/ppermute | solution.py:373
  80.6 46.6 %all-to-all-start.2 = ((bf16[32,96,256]{2,1,0:T(8,128)(2,1)}), bf16[32,96,256]{2,1,0:T(8,128)(2,1)S(1)}, u32[]{:S(2)}, u32[]{:S(2)}) async-start(bf16[32,96,256]{2,1,0:T(8,128)(2,1)} %bitcast.53), calls=%async_computation.2 | async-start | bytes 3145728 | tf_op jit(solution)/shard_map/cond/branch_0_fun/all_to_all | solution.py:361
  85.4 30.7 %collective-permute-start.10 = (f32[3,7,512]{2,1,0:T(8,128)S(1)}, f32[3,7,512]{2,1,0:T(8,128)S(1)}, u32[]{:S(2)}, u32[]{:S(2)}) collective-permute-start(f32[3,7,512]{2,1,0:T(8,128)S(1)} %pad_maximum_fusion.refs_0_), channel_id=1, source_target_pairs={{0,24},{4,28},{8,16},{12,20},{16,8},{20,12},{24,0},{28,4},{1,25},{... | collective-permute-start | bytes 129032 | tf_op jit(solution)/shard_map/cond/branch_0_fun/ppermute | solution.py:373
  89.1 37.5 %collective-permute-start.9 = (f32[3,7,512]{2,1,0:T(8,128)S(1)}, f32[3,7,512]{2,1,0:T(8,128)S(1)}, u32[]{:S(2)}, u32[]{:S(2)}) collective-permute-start(f32[3,7,512]{2,1,0:T(8,128)S(1)} %pad_maximum_fusion.refs_0_), channel_id=1, source_target_pairs={{0,16},{4,20},{8,24},{12,28},{16,0},{20,4},{24,8},{28,12},{1,17},{... | collective-permute-start | bytes 129032 | tf_op jit(solution)/shard_map/cond/branch_0_fun/ppermute | solution.py:373
  89.1 37.5 %collective-permute-start.8 = (f32[3,7,512]{2,1,0:T(8,128)S(1)}, f32[3,7,512]{2,1,0:T(8,128)S(1)}, u32[]{:S(2)}, u32[]{:S(2)}) collective-permute-start(f32[3,7,512]{2,1,0:T(8,128)S(1)} %pad_maximum_fusion.refs_0_), channel_id=1, source_target_pairs={{0,8},{4,12},{8,0},{12,4},{16,24},{20,28},{24,16},{28,20},{1,9},{5... | collective-permute-start | bytes 129032 | tf_op jit(solution)/shard_map/cond/branch_0_fun/ppermute | solution.py:373
where the time goes:
time: 129 us; the launch traced here: 128 us
  waiting for transfers between devices  65.1 us (50%)
  starting transfers between devices  39 us (30%)
  Pallas kernels  20.2 us (16%)
  local copies, waits for them, and re-layouts  2.07 us (2%)
  between operations  1.93 us (1%)
    ppermute x11, waiting for transfers between devices, across(): return lax.ppermute(value, 'ctx', [(i, i ^ step) for i in range(count)])  50.6 us
    ppermute x11, starting transfers between devices, across(): return lax.ppermute(value, 'ctx', [(i, i ^ step) for i in range(count)])  24.2 us
    all_to_all x3, starting transfers between devices, swap(): lax.all_to_all(value.reshape(shape[0], -1, shape[-1]), axes, split_axis=0...  14.8 us
    all_to_all x3, waiting for transfers between devices, swap(): lax.all_to_all(value.reshape(shape[0], -1, shape[-1]), axes, split_axis=0...  14.6 us
    pallas_call x1, Pallas kernels, backward(): pl.pallas_call(backward_kernel, grid_spec=pltpu.PrefetchScalarGridSpec(nu...  6.56 us
    pallas_call x1, Pallas kernels, forward(): pl.pallas_call(forward_kernel, grid_spec=pltpu.PrefetchScalarGridSpec(num...  6.19 us
  transfers between devices with their start and end apart: 14, of which 6 were waited for; matrix products, arithmetic and copies ran while one was open for 1% of the time, Pallas kernels for 13%

commit v1 on v0

--- a/solution.py
+++ b/solution.py
@@ -214,7 +214,7 @@
 def backward_kernel(
     local, x_ref, before_ref, mixed_ref, prob_ref, att_ref, *refs
 ):
-    *up_refs, cgrad_ref, tapg_ref, head_ref, up_ref = refs
+    *up_refs, cgrad_ref, extra_ref, up_ref = refs
     sources, streams, rows, _ = x_ref.shape
     tokens = sources * rows
     per = att_ref.shape[1]
@@ -268,7 +268,8 @@
             if span.start < own.start:
                 cgrad[m, outs, :] += part[: own.start - span.start]
             cgrad[m, out, :] = part[own.start - span.start :]
-    head_ref[:, :, lanes] = cgrad[:, PAD : 2 * PAD, :]
+    extra_ref[:, 0:PAD, lanes] = cgrad[:, PAD : 2 * PAD, :]
+    extra_ref[:, PAD + KW :, lanes] = edge[:, KW:]
     span = BLOCK // rows
     for m in range(streams):
         early = before_ref[m, :, lanes].astype(jnp.float32)
@@ -280,7 +281,9 @@
                 product = here * cgrad[m, PAD + start + lag : PAD + start + lag + BLOCK, :]
                 sums[lag] = sums[lag] + jnp.sum(product.reshape(BLOCK // 8, 8, HEAD_DIM), axis=0)
         for lag in range(KW):
-            tapg_ref[m, lag : lag + 1, lanes] = jnp.sum(sums[lag], axis=0, keepdims=True)
+            extra_ref[m, PAD + lag : PAD + lag + 1, lanes] = jnp.sum(
+                sums[lag], axis=0, keepdims=True
+            )
 
 
 def backward(local, x, before, mixed, prob, att, pieces):
@@ -303,13 +306,12 @@
                 pl.BlockSpec((members, tokens // members, HEAD_DIM), lambda h, p: (0, 0, h)),
             ]
             + [here] * members,
-            out_specs=[here, here, here],
+            out_specs=[here, here],
             scratch_shapes=[pltpu.VMEM((members, tokens // members, width), jnp.bfloat16)],
         ),
         out_shape=[
             jax.ShapeDtypeStruct((per, streams, tokens + 2 * PAD, HEAD_DIM), jnp.float32),
-            jax.ShapeDtypeStruct((streams, KW, width), jnp.float32),
-            jax.ShapeDtypeStruct((streams, PAD, width), jnp.float32),
+            jax.ShapeDtypeStruct((streams, 2 * PAD, width), jnp.float32),
         ],
         compiler_params=room(BACK),
         cost_estimate=estimate(20_000_000_000, 12 * x.size),
@@ -373,12 +375,10 @@
     return lax.ppermute(value, "ctx", [(i, i ^ step) for i in range(count)])
 
 
-def first_exchange(piece, members):
-    if members < lax.axis_size("ctx"):
-        return 1, piece + across(piece, members)
+def beside_neighbour(piece):
     other = across(piece, 1)
     even = lax.axis_index("ctx") % 2 == 0
-    return 2, jnp.concatenate(
+    return jnp.concatenate(
         [jnp.where(even, piece, other), jnp.where(even, other, piece)], axis=-1
     )
 
@@ -393,7 +393,9 @@
         o_ref = refs[-1]
         for step in steps:
             column = lax.rem(position_ref[0] ^ step, members) // span
-            o_ref[:, :, pl.ds(pl.multiple_of(column * wide, wide), wide)] = refs[step // span][...]
+            o_ref[:, :, pl.ds(pl.multiple_of(column * wide, wide), wide)] = refs[step // span][
+                ...
+            ].astype(jnp.float32)
 
     columns = members // span * wide
     return pl.pallas_call(
@@ -404,7 +406,7 @@
             in_specs=[pl.BlockSpec((streams, taps, wide), lambda i, p: (0, 0, 0))] * len(pieces),
             out_specs=pl.BlockSpec((streams, taps, columns), lambda i, p: (0, 0, 0)),
         ),
-        out_shape=jax.ShapeDtypeStruct((streams, taps, columns), held.dtype),
+        out_shape=jax.ShapeDtypeStruct((streams, taps, columns), jnp.float32),
         compiler_params=room(4),
         name="place_columns",
     )(position.reshape(1), *pieces)
@@ -436,11 +438,15 @@
     mixed, prob, att = forward(doc_ids, x, taps, before, members)
     attended = join_columns(swap(att, "ctx", every)[:, None, None])[0]
     away = [pltpu.with_memory_space_constraint(v, pltpu.HBM) for v in (mixed, prob, att)]
-    cgrad, tap_grad, head = backward(local, x, before, *away, pieces)
-    span, held = first_exchange(tap_grad, members)
+    cgrad, extra = backward(local, x, before, *away, pieces)
+    if parts > 1:
+        other = across(extra, members)
+        span, held = 1, (extra + other)[:, PAD : PAD + KW].astype(jnp.bfloat16)
+    else:
+        span, held = 2, beside_neighbour(extra[:, PAD : PAD + KW].astype(jnp.bfloat16))
     grad, tail = spread(cgrad, taps, rows)
     if parts > 1:
-        after = lax.ppermute(head, "ctx", [(to, source) for source, to in upward])
+        after = jnp.where(position < members, other[:, 0:PAD], 0.0)
         after = jnp.concatenate([jnp.zeros_like(after), after], axis=1)
         for lag in range(KW):
             tail = tail + taps[:, lag : lag + 1] * after[:, lag : lag + PAD]

time: 129 us -> 127 us (0.984)
  waiting for transfers between devices: 65.1 us -> 63.1 us
    ppermute x11, waiting for transfers between devices: 50.6 us -> 48.5 us  [across(): return lax.ppermute(value, 'ctx', [(i, i ^ step) for i in range(count)])]
where the time goes in v1:
time: 127 us; the launch traced here: 126 us
  waiting for transfers between devices  63.1 us (50%)
  starting transfers between devices  38.9 us (31%)
  Pallas kernels  20.2 us (16%)
  local copies, waits for them, and re-layouts  2.07 us (2%)
  between operations  1.93 us (2%)
    ppermute x11, waiting for transfers between devices, across(): return lax.ppermute(value, 'ctx', [(i, i ^ step) for i in range(count)])  48.5 us
    ppermute x11, starting transfers between devices, across(): return lax.ppermute(value, 'ctx', [(i, i ^ step) for i in range(count)])  24.2 us
    all_to_all x3, starting transfers between devices, swap(): lax.all_to_all(value.reshape(shape[0], -1, shape[-1]), axes, split_axis=0...  14.8 us
    all_to_all x3, waiting for transfers between devices, swap(): lax.all_to_all(value.reshape(shape[0], -1, shape[-1]), axes, split_axis=0...  14.6 us
    pallas_call x1, Pallas kernels, backward(): pl.pallas_call(backward_kernel, grid_spec=pltpu.PrefetchScalarGridSpec(nu...  6.52 us
    pallas_call x1, Pallas kernels, forward(): pl.pallas_call(forward_kernel, grid_spec=pltpu.PrefetchScalarGridSpec(num...  6.19 us
  transfers between devices with their start and end apart: 14, of which 6 were waited for; matrix products, arithmetic and copies ran while one was open for 1% of the time, Pallas kernels for 13%

profile of v1, /device:TPU:0, one launch (start us, length us, event | category | flops | bytes accessed | tf_op | source)
XLA Modules:
  0.0 126.4 jit_solution(14540082223613959587)
XLA Ops:
  0.6 1.3 %fusion.14 = (s32[1]{0:T(128)}, s32[1]{0:T(128)}) fusion(s32[8]{0:T(128)} %param.10), kind=kLoop, calls=%fused_computation.44 | loop fusion | bytes 16 | tf_op jit(solution)/shard_map/slice | solution.py:581
  3.2 123.1 %conditional.1 = (bf16[128,2048]{1,0:T(8,128)(2,1)}, bf16[32,3,8192]{2,0,1:T(8,128)(2,1)}, f32[3,7,2048]{2,1,0:T(8,128)}) conditional(s32[]{:T(128)} %bitcast.22, (bf16[32,3,8192]{2,0,1:T(8,128)(2,1)}, f32[3,7,2048]{2,1,0:T(8,128)}, s32[8]{0:T(128)}, bf16[128,2048]{1,0:T(8,128)(2,1)}) %tuple.23, (bf16[32,3,8192]{2,0,1:T(8,128)(2,1)}, s32[8]{0:T(128)}, ...), branch_computations={%region_0.1_spmd, %region_1.2_spmd} | conditional | flops 32000208896 | bytes 45092924 | solution.py:582
  3.3 2.3 %split_columns.2 = bf16[8,4,3,32,256]{4,3,2,1,0:T(8,128)(2,1)} custom-call(bf16[3,32,8192]{2,1,0:T(8,128)(2,1)} %bitcast.49), custom_call_target="tpu_custom_call" | custom-call | bytes 3145728 | tf_op jit(solution)/shard_map/cond/branch_0_fun/split_columns/pallas_call | solution.py:46
  5.6 0.0 copy-start
  5.6 0.0 copy-start.2
  5.6 7.3 %all-to-all-start = ((bf16[32,96,256]{2,1,0:T(8,128)(2,1)}), bf16[32,96,256]{2,1,0:T(8,128)(2,1)S(1)}, u32[]{:S(2)}, u32[]{:S(2)}) async-start(bf16[32,96,256]{2,1,0:T(8,128)(2,1)} %bitcast.51), calls=%async_computation | async-start | bytes 3145728 | tf_op jit(solution)/shard_map/cond/branch_0_fun/all_to_all | solution.py:363
  12.9 0.0 copy-done
  12.9 0.1 split_rows.2
  13.0 1.8 %collective-permute-start = (bf16[128,256]{1,0:T(8,128)(2,1)S(1)}, bf16[128,256]{1,0:T(8,128)(2,1)S(1)}, u32[]{:S(2)}, u32[]{:S(2)}) collective-permute-start(bf16[128,256]{1,0:T(8,128)(2,1)S(1)} %get-tuple-element.36), channel_id=1, source_target_pairs={{0,4},{4,0},{8,12},{12,8},{16,20},{20,16},{24,28},{28,24},{1,5},{5... | collective-permute-start | bytes 196616 | tf_op jit(solution)/shard_map/cond/branch_0_fun/ppermute | solution.py:375
  14.8 1.5 %collective-permute-start.1 = (bf16[128,256]{1,0:T(8,128)(2,1)S(1)}, bf16[128,256]{1,0:T(8,128)(2,1)S(1)}, u32[]{:S(2)}, u32[]{:S(2)}) collective-permute-start(bf16[128,256]{1,0:T(8,128)(2,1)S(1)} %get-tuple-element.37), channel_id=1, source_target_pairs={{0,8},{4,12},{8,0},{12,4},{16,24},{20,28},{24,16},{28,20},{1,9},{5... | collective-permute-start | bytes 196616 | tf_op jit(solution)/shard_map/cond/branch_0_fun/ppermute | solution.py:375
  16.3 0.3 collective-permute-start.2
  16.6 2.7 %collective-permute-start.3 = (bf16[128,256]{1,0:T(8,128)(2,1)S(1)}, bf16[128,256]{1,0:T(8,128)(2,1)S(1)}, u32[]{:S(2)}, u32[]{:S(2)}) collective-permute-start(bf16[128,256]{1,0:T(8,128)(2,1)S(1)} %get-tuple-element.39), channel_id=1, source_target_pairs={{0,16},{4,20},{8,24},{12,28},{16,0},{20,4},{24,8},{28,12},{1,17},{... | collective-permute-start | bytes 196616 | tf_op jit(solution)/shard_map/cond/branch_0_fun/ppermute | solution.py:375
  19.2 1.5 %collective-permute-start.4 = (bf16[128,256]{1,0:T(8,128)(2,1)S(1)}, bf16[128,256]{1,0:T(8,128)(2,1)S(1)}, u32[]{:S(2)}, u32[]{:S(2)}) collective-permute-start(bf16[128,256]{1,0:T(8,128)(2,1)S(1)} %get-tuple-element.40), channel_id=1, source_target_pairs={{0,20},{4,16},{8,28},{12,24},{16,4},{20,0},{24,12},{28,8},{1,21},{... | collective-permute-start | bytes 196616 | tf_op jit(solution)/shard_map/cond/branch_0_fun/ppermute | solution.py:375
  20.7 0.7 constant_dynamic-slice_fusion.taps_ref
  21.4 1.5 %collective-permute-done.refs_1_ = bf16[128,256]{1,0:T(8,128)(2,1)S(1)} collective-permute-done((bf16[128,256]{1,0:T(8,128)(2,1)S(1)}, bf16[128,256]{1,0:T(8,128)(2,1)S(1)}, u32[]{:S(2)}, u32[]{:S(2)}) %collective-permute-start) | collective-permute-done | bytes 65568 | tf_op jit(solution)/shard_map/cond/branch_0_fun/ppermute | solution.py:375
  22.9 5.7 %collective-permute-start.5 = (bf16[128,256]{1,0:T(8,128)(2,1)S(1)}, bf16[128,256]{1,0:T(8,128)(2,1)S(1)}, u32[]{:S(2)}, u32[]{:S(2)}) collective-permute-start(bf16[128,256]{1,0:T(8,128)(2,1)S(1)} %get-tuple-element.41), channel_id=1, source_target_pairs={{0,24},{4,28},{8,16},{12,20},{16,8},{20,12},{24,0},{28,4},{1,25},{... | collective-permute-start | bytes 196616 | tf_op jit(solution)/shard_map/cond/branch_0_fun/ppermute | solution.py:375
  28.7 12.3 %collective-permute-done.1.refs_2_ = bf16[128,256]{1,0:T(8,128)(2,1)S(1)} collective-permute-done((bf16[128,256]{1,0:T(8,128)(2,1)S(1)}, bf16[128,256]{1,0:T(8,128)(2,1)S(1)}, u32[]{:S(2)}, u32[]{:S(2)}) %collective-permute-start.1) | collective-permute-done | bytes 65568 | tf_op jit(solution)/shard_map/cond/branch_0_fun/ppermute | solution.py:375
  41.0 4.4 %collective-permute-start.6 = (bf16[128,256]{1,0:T(8,128)(2,1)S(1)}, bf16[128,256]{1,0:T(8,128)(2,1)S(1)}, u32[]{:S(2)}, u32[]{:S(2)}) collective-permute-start(bf16[128,256]{1,0:T(8,128)(2,1)S(1)} %get-tuple-element.42), channel_id=1, source_target_pairs={{0,28},{4,24},{8,20},{12,16},{16,12},{20,8},{24,4},{28,0},{1,29},{... | collective-permute-start | bytes 196616 | tf_op jit(solution)/shard_map/cond/branch_0_fun/ppermute | solution.py:375
  45.4 11.3 %all-to-all-done = bf16[32,96,256]{2,1,0:T(8,128)(2,1)S(1)} async-done(((bf16[32,96,256]{2,1,0:T(8,128)(2,1)}), bf16[32,96,256]{2,1,0:T(8,128)(2,1)S(1)}, u32[]{:S(2)}, u32[]{:S(2)}) %all-to-all-start) | async-done | bytes 1572896 | tf_op jit(solution)/shard_map/cond/branch_0_fun/all_to_all | solution.py:363
  56.7 0.0 copy-done.2
  56.7 6.2 %forward.2 = (bf16[2,3,1024,128]{3,2,1,0:T(8,128)(2,1)}, f32[2,30,128,128]{3,2,1,0:T(8,128)}, bf16[8,128,256]{2,1,0:T(8,128)(2,1)}) custom-call(s32[8]{0:T(128)S(1)} %copy-done.2, bf16[32,3,32,256]{3,2,1,0:T(8,128)(2,1)S(1)} %bitcast.47, f32[3,7,256]{2,1,0:T(8,128)S(1)} %constant_dynamic-slice_fusion.taps_ref, ...), custom_call_target="tpu_custom_call" | custom-call | flops 10000000000 | bytes 6291456 | tf_op jit(solution)/shard_map/cond/branch_0_fun/forward/pallas_call | solution.py:190
  62.9 3.5 %all-to-all-start.1 = ((bf16[8,128,256]{2,1,0:T(8,128)(2,1)}), bf16[8,128,256]{2,1,0:T(8,128)(2,1)S(1)}, u32[]{:S(2)}, u32[]{:S(2)}) async-start(bf16[8,128,256]{2,1,0:T(8,128)(2,1)} %get-tuple-element.33.att_ref), calls=%async_computation.1 | async-start | bytes 1048576 | tf_op jit(solution)/shard_map/cond/branch_0_fun/all_to_all | solution.py:363
  66.4 0.0 collective-permute-done.2.refs_3_
  66.4 0.0 collective-permute-done.3.refs_4_
  66.5 0.0 collective-permute-done.4.refs_5_
  66.5 0.0 collective-permute-done.5.refs_6_
  66.5 0.0 collective-permute-done.6.refs_7_
  66.5 6.5 %backward.2 = (f32[2,3,1040,128]{3,2,1,0:T(8,128)S(1)}, f32[3,16,256]{2,1,0:T(8,128)S(1)}) custom-call(s32[1]{0:T(128)} %bitcast.local_ref.local, bf16[32,3,32,256]{3,2,1,0:T(8,128)(2,1)S(1)} %bitcast.48, bf16[3,8,256]{2,1,0:T(8,128)(2,1)S(1)} %broadcast_1_before_ref.0.before_ref, bf16[2,3,1024,128]{3,2,1,0:T(8,128)(2,1)} %get-tuple-element.31.mixed_ref, ...), custom_call_target="tpu_custom_call" | custom-call | flops 20000000000 | bytes 9437184 | tf_op jit(solution)/shard_map/cond/branch_0_fun/backward/pallas_call | solution.py:296
  73.0 2.0 %collective-permute-start.7 = (bf16[3,7,256]{2,1,0:T(8,128)(2,1)S(1)}, bf16[3,7,256]{2,1,0:T(8,128)(2,1)S(1)}, u32[]{:S(2)}, u32[]{:S(2)}) collective-permute-start(bf16[3,7,256]{2,1,0:T(8,128)(2,1)S(1)} %slice.157), channel_id=1, source_target_pairs={{0,4},{4,0},{8,12},{12,8},{16,20},{20,16},{24,28},{28,24},{1,5},{5... | collective-permute-start | bytes 32264 | tf_op jit(solution)/shard_map/cond/branch_0_fun/ppermute | solution.py:375
  75.0 2.3 %spread.2 = (bf16[32,3,32,256]{3,2,1,0:T(8,128)(2,1)}, f32[3,8,256]{2,1,0:T(8,128)}) custom-call(f32[2,3,1040,128]{3,2,1,0:T(8,128)S(1)} %get-tuple-element.43.cgrad_ref, f32[3,7,256]{2,1,0:T(8,128)S(1)} %constant_dynamic-slice_fusion.taps_ref), custom_call_target="tpu_custom_call" | custom-call | flops 2000000000 | bytes 4792320 | tf_op jit(solution)/shard_map/cond/branch_0_fun/spread/pallas_call | solution.py:343
  77.3 0.0 collective-permute-done.7
  77.3 3.3 %all-to-all-done.1 = bf16[8,128,256]{2,1,0:T(8,128)(2,1)S(1)} async-done(((bf16[8,128,256]{2,1,0:T(8,128)(2,1)}), bf16[8,128,256]{2,1,0:T(8,128)(2,1)S(1)}, u32[]{:S(2)}, u32[]{:S(2)}) %all-to-all-start.1) | async-done | bytes 524320 | tf_op jit(solution)/shard_map/cond/branch_0_fun/all_to_all | solution.py:363
  80.6 4.0 %all-to-all-start.2 = ((bf16[32,96,256]{2,1,0:T(8,128)(2,1)}), bf16[32,96,256]{2,1,0:T(8,128)(2,1)S(1)}, u32[]{:S(2)}, u32[]{:S(2)}) async-start(bf16[32,96,256]{2,1,0:T(8,128)(2,1)} %bitcast.53), calls=%async_computation.2 | async-start | bytes 3145728 | tf_op jit(solution)/shard_map/cond/branch_0_fun/all_to_all | solution.py:363
  84.6 0.8 join_columns.4
  85.4 3.6 %collective-permute-start.10 = (bf16[3,7,512]{2,1,0:T(8,128)(2,1)S(1)}, bf16[3,7,512]{2,1,0:T(8,128)(2,1)S(1)}, u32[]{:S(2)}, u32[]{:S(2)}) collective-permute-start(bf16[3,7,512]{2,1,0:T(8,128)(2,1)S(1)} %pad_maximum_fusion.refs_0_), channel_id=1, source_target_pairs={{0,24},{4,28},{8,16},{12,20},{16,8},{20,12},{24,0},{28,4},{1,25},{... | collective-permute-start | bytes 64520 | tf_op jit(solution)/shard_map/cond/branch_0_fun/ppermute | solution.py:375
  89.1 0.0 collective-permute-start.9
  89.1 0.8 collective-permute-start.8
  89.8 25.8 %collective-permute-done.10.refs_3_ = bf16[3,7,512]{2,1,0:T(8,128)(2,1)S(1)} collective-permute-done((bf16[3,7,512]{2,1,0:T(8,128)(2,1)S(1)}, bf16[3,7,512]{2,1,0:T(8,128)(2,1)S(1)}, u32[]{:S(2)}, u32[]{:S(2)}) %collective-permute-start.10) | collective-permute-done | bytes 21536 | tf_op jit(solution)/shard_map/cond/branch_0_fun/ppermute | solution.py:375
  115.6 8.8 %collective-permute-done.9.refs_2_ = bf16[3,7,512]{2,1,0:T(8,128)(2,1)S(1)} collective-permute-done((bf16[3,7,512]{2,1,0:T(8,128)(2,1)S(1)}, bf16[3,7,512]{2,1,0:T(8,128)(2,1)S(1)}, u32[]{:S(2)}, u32[]{:S(2)}) %collective-permute-start.9) | collective-permute-done | bytes 21536 | tf_op jit(solution)/shard_map/cond/branch_0_fun/ppermute | solution.py:375
  124.4 0.0 collective-permute-done.8.refs_1_
  124.4 0.7 place_columns.2
  125.1 0.0 all-to-all-done.2
  125.1 1.2 join_columns.5
  (4 shorter events, 0.0 us)
Async XLA Ops:
  5.6 7.3 %copy-start = (bf16[128,2048]{1,0:T(8,128)(2,1)S(1)}, bf16[128,2048]{1,0:T(8,128)(2,1)}, u32[]{:S(2)}) copy-start(bf16[128,2048]{1,0:T(8,128)(2,1)} %get-tuple-element.34.x_ref) | copy-start | bytes 1572868 | tf_op jit(solution)/shard_map/cond
  5.6 51.1 %copy-start.2 = (s32[8]{0:T(128)S(1)}, s32[8]{0:T(128)}, u32[]{:S(2)}) copy-start(s32[8]{0:T(128)} %get-tuple-element.29.docs) | copy-start | bytes 100 | tf_op jit(solution)/shard_map/cond
  5.6 51.1 %all-to-all-start = ((bf16[32,96,256]{2,1,0:T(8,128)(2,1)}), bf16[32,96,256]{2,1,0:T(8,128)(2,1)S(1)}, u32[]{:S(2)}, u32[]{:S(2)}) async-start(bf16[32,96,256]{2,1,0:T(8,128)(2,1)} %bitcast.51), calls=%async_computation | async-start | bytes 3145728 | tf_op jit(solution)/shard_map/cond/branch_0_fun/all_to_all | solution.py:363
  13.0 9.9 %collective-permute-start = (bf16[128,256]{1,0:T(8,128)(2,1)S(1)}, bf16[128,256]{1,0:T(8,128)(2,1)S(1)}, u32[]{:S(2)}, u32[]{:S(2)}) collective-permute-start(bf16[128,256]{1,0:T(8,128)(2,1)S(1)} %get-tuple-element.36), channel_id=1, source_target_pairs={{0,4},{4,0},{8,12},{12,8},{16,20},{20,16},{24,28},{28,24},{1,5},{5... | collective-permute-start | bytes 196616 | tf_op jit(solution)/shard_map/cond/branch_0_fun/ppermute | solution.py:375
  14.8 26.2 %collective-permute-start.1 = (bf16[128,256]{1,0:T(8,128)(2,1)S(1)}, bf16[128,256]{1,0:T(8,128)(2,1)S(1)}, u32[]{:S(2)}, u32[]{:S(2)}) collective-permute-start(bf16[128,256]{1,0:T(8,128)(2,1)S(1)} %get-tuple-element.37), channel_id=1, source_target_pairs={{0,8},{4,12},{8,0},{12,4},{16,24},{20,28},{24,16},{28,20},{1,9},{5... | collective-permute-start | bytes 196616 | tf_op jit(solution)/shard_map/cond/branch_0_fun/ppermute | solution.py:375
  16.3 50.1 %collective-permute-start.2 = (bf16[128,256]{1,0:T(8,128)(2,1)S(1)}, bf16[128,256]{1,0:T(8,128)(2,1)S(1)}, u32[]{:S(2)}, u32[]{:S(2)}) collective-permute-start(bf16[128,256]{1,0:T(8,128)(2,1)S(1)} %get-tuple-element.38), channel_id=1, source_target_pairs={{0,12},{4,8},{8,4},{12,0},{16,28},{20,24},{24,20},{28,16},{1,13},{... | collective-permute-start | bytes 196616 | tf_op jit(solution)/shard_map/cond/branch_0_fun/ppermute | solution.py:375
  16.6 49.9 %collective-permute-start.3 = (bf16[128,256]{1,0:T(8,128)(2,1)S(1)}, bf16[128,256]{1,0:T(8,128)(2,1)S(1)}, u32[]{:S(2)}, u32[]{:S(2)}) collective-permute-start(bf16[128,256]{1,0:T(8,128)(2,1)S(1)} %get-tuple-element.39), channel_id=1, source_target_pairs={{0,16},{4,20},{8,24},{12,28},{16,0},{20,4},{24,8},{28,12},{1,17},{... | collective-permute-start | bytes 196616 | tf_op jit(solution)/shard_map/cond/branch_0_fun/ppermute | solution.py:375
  19.2 47.2 %collective-permute-start.4 = (bf16[128,256]{1,0:T(8,128)(2,1)S(1)}, bf16[128,256]{1,0:T(8,128)(2,1)S(1)}, u32[]{:S(2)}, u32[]{:S(2)}) collective-permute-start(bf16[128,256]{1,0:T(8,128)(2,1)S(1)} %get-tuple-element.40), channel_id=1, source_target_pairs={{0,20},{4,16},{8,28},{12,24},{16,4},{20,0},{24,12},{28,8},{1,21},{... | collective-permute-start | bytes 196616 | tf_op jit(solution)/shard_map/cond/branch_0_fun/ppermute | solution.py:375
  22.9 43.5 %collective-permute-start.5 = (bf16[128,256]{1,0:T(8,128)(2,1)S(1)}, bf16[128,256]{1,0:T(8,128)(2,1)S(1)}, u32[]{:S(2)}, u32[]{:S(2)}) collective-permute-start(bf16[128,256]{1,0:T(8,128)(2,1)S(1)} %get-tuple-element.41), channel_id=1, source_target_pairs={{0,24},{4,28},{8,16},{12,20},{16,8},{20,12},{24,0},{28,4},{1,25},{... | collective-permute-start | bytes 196616 | tf_op jit(solution)/shard_map/cond/branch_0_fun/ppermute | solution.py:375
  41.0 25.5 %collective-permute-start.6 = (bf16[128,256]{1,0:T(8,128)(2,1)S(1)}, bf16[128,256]{1,0:T(8,128)(2,1)S(1)}, u32[]{:S(2)}, u32[]{:S(2)}) collective-permute-start(bf16[128,256]{1,0:T(8,128)(2,1)S(1)} %get-tuple-element.42), channel_id=1, source_target_pairs={{0,28},{4,24},{8,20},{12,16},{16,12},{20,8},{24,4},{28,0},{1,29},{... | collective-permute-start | bytes 196616 | tf_op jit(solution)/shard_map/cond/branch_0_fun/ppermute | solution.py:375
  62.9 17.7 %all-to-all-start.1 = ((bf16[8,128,256]{2,1,0:T(8,128)(2,1)}), bf16[8,128,256]{2,1,0:T(8,128)(2,1)S(1)}, u32[]{:S(2)}, u32[]{:S(2)}) async-start(bf16[8,128,256]{2,1,0:T(8,128)(2,1)} %get-tuple-element.33.att_ref), calls=%async_computation.1 | async-start | bytes 1048576 | tf_op jit(solution)/shard_map/cond/branch_0_fun/all_to_all | solution.py:363
  73.0 4.3 %collective-permute-start.7 = (bf16[3,7,256]{2,1,0:T(8,128)(2,1)S(1)}, bf16[3,7,256]{2,1,0:T(8,128)(2,1)S(1)}, u32[]{:S(2)}, u32[]{:S(2)}) collective-permute-start(bf16[3,7,256]{2,1,0:T(8,128)(2,1)S(1)} %slice.157), channel_id=1, source_target_pairs={{0,4},{4,0},{8,12},{12,8},{16,20},{20,16},{24,28},{28,24},{1,5},{5... | collective-permute-start | bytes 32264 | tf_op jit(solution)/shard_map/cond/branch_0_fun/ppermute | solution.py:375
  80.6 44.5 %all-to-all-start.2 = ((bf16[32,96,256]{2,1,0:T(8,128)(2,1)}), bf16[32,96,256]{2,1,0:T(8,128)(2,1)S(1)}, u32[]{:S(2)}, u32[]{:S(2)}) async-start(bf16[32,96,256]{2,1,0:T(8,128)(2,1)} %bitcast.53), calls=%async_computation.2 | async-start | bytes 3145728 | tf_op jit(solution)/shard_map/cond/branch_0_fun/all_to_all | solution.py:363
  85.4 30.2 %collective-permute-start.10 = (bf16[3,7,512]{2,1,0:T(8,128)(2,1)S(1)}, bf16[3,7,512]{2,1,0:T(8,128)(2,1)S(1)}, u32[]{:S(2)}, u32[]{:S(2)}) collective-permute-start(bf16[3,7,512]{2,1,0:T(8,128)(2,1)S(1)} %pad_maximum_fusion.refs_0_), channel_id=1, source_target_pairs={{0,24},{4,28},{8,16},{12,20},{16,8},{20,12},{24,0},{28,4},{1,25},{... | collective-permute-start | bytes 64520 | tf_op jit(solution)/shard_map/cond/branch_0_fun/ppermute | solution.py:375
  89.1 35.4 %collective-permute-start.9 = (bf16[3,7,512]{2,1,0:T(8,128)(2,1)S(1)}, bf16[3,7,512]{2,1,0:T(8,128)(2,1)S(1)}, u32[]{:S(2)}, u32[]{:S(2)}) collective-permute-start(bf16[3,7,512]{2,1,0:T(8,128)(2,1)S(1)} %pad_maximum_fusion.refs_0_), channel_id=1, source_target_pairs={{0,16},{4,20},{8,24},{12,28},{16,0},{20,4},{24,8},{28,12},{1,17},{... | collective-permute-start | bytes 64520 | tf_op jit(solution)/shard_map/cond/branch_0_fun/ppermute | solution.py:375
  89.1 35.4 %collective-permute-start.8 = (bf16[3,7,512]{2,1,0:T(8,128)(2,1)S(1)}, bf16[3,7,512]{2,1,0:T(8,128)(2,1)S(1)}, u32[]{:S(2)}, u32[]{:S(2)}) collective-permute-start(bf16[3,7,512]{2,1,0:T(8,128)(2,1)S(1)} %pad_maximum_fusion.refs_0_), channel_id=1, source_target_pairs={{0,8},{4,12},{8,0},{12,4},{16,24},{20,28},{24,16},{28,20},{1,9},{5... | collective-permute-start | bytes 64520 | tf_op jit(solution)/shard_map/cond/branch_0_fun/ppermute | solution.py:375
